TPU v7x, 1024 devices: a whole 8x8x8 slice. The times are simulated.
1024 devices in a mesh: img: 16 (over y, core), seq: 64 (over x, z).
Axes of the slice: x: 8, y: 8, z: 8, core: 2. Of those that a mesh axis runs over, the one named last changes fastest.
Arguments:
- llm_grads: bfloat16 [16, 2048, 8192], P('img', 'seq'), may hold values from -6 to 6
- token_target: int32 [16, 2048], P('img', 'seq'), may hold values from 0 to 2047, as said below
- patches: bfloat16 [16, 8192, 1280], P('img', 'seq'), may hold values from -150 to 150
- gain: float32 [1280], replicated, may hold values from 0.5 to 1.5
- w_down: bfloat16 [5120, 8192], P(None, 'img'), may hold values from -0.078125 to 0.078125
- queries: bfloat16 [16, 8192, 1280], P('img', 'seq'), may hold values from -40 to 40
- keys: bfloat16 [16, 8192, 1280], P('img', 'seq'), may hold values from -5 to 5
- values: bfloat16 [16, 8192, 1280], P('img', 'seq'), may hold values from -5 to 5
- window_ids: int32 [16, 64, 32], P('img', 'seq'), may hold values from 0 to 3, never falling along the last dimension, each value on 1 to 16 neighbouring positions
Outputs:
- grad_q: bfloat16 [16, 8192, 1280], P('img', 'seq')
- grad_k: bfloat16 [16, 8192, 1280], P('img', 'seq')
- grad_v: bfloat16 [16, 8192, 1280], P('img', 'seq')
- gain_grad: float32 [1280], replicated
- bias_grad: float32 [8192], replicated
Inputs may be any that keep to these rules, and one draw needn't show every extreme that they name: In each group i, token_target[i] is a permutation: position s * 32 + j (held by index s of seq) holds merged token d * 32 + m (held by index d of seq). At most 1 position of one seq index holds a merged token of any one seq index, and in every group some pair of seq indices has exactly 1.
All inputs are finite; a program needn't handle non-finite values.
Results may differ from a plain program's by a relative error of at most 0.024.
Values may be sent and summed in bfloat16 or wider, within the bound.
A program may use at most 64 MiB of HBM per device.

v0:
```python
import math

import jax
import jax.numpy as jnp
from jax import lax
from jax.sharding import PartitionSpec as P

HEADS = 16
HEAD_DIM = 80


def earlier_equal(labels, order_key):
    same_label = labels[:, None] == labels[None, :]
    earlier = order_key[None, :] < order_key[:, None]
    return jnp.sum(jnp.logical_and(same_label, earlier), axis=1)


def pack_rows(row_values, targets, peer_count, capacity):
    row_count = row_values.shape[0]
    destination = targets // row_count
    local_row = targets % row_count
    slot_index = destination * capacity + earlier_equal(
        destination, jnp.arange(row_count, dtype=jnp.int32)
    )
    matches = slot_index[None, :] == jnp.arange(peer_count * capacity, dtype=jnp.int32)[:, None]
    selector = matches.astype(row_values.dtype)
    packed = jnp.dot(selector, row_values, preferred_element_type=jnp.float32).astype(
        row_values.dtype
    )
    slot_rows = jnp.sum(jnp.where(matches, local_row[None, :] + 1, 0), axis=1) - 1
    slot_labels = slot_rows.astype(jnp.float32).astype(jnp.bfloat16).reshape(peer_count, capacity)
    return (packed.reshape(peer_count, capacity, row_values.shape[1]), slot_labels)


def unpack_rows(received, slot_labels, row_count):
    flat_rows = received.reshape(-1, received.shape[2])
    flat_labels = slot_labels.reshape(-1).astype(jnp.float32).astype(jnp.int32)
    selector = (flat_labels[None, :] == jnp.arange(row_count, dtype=jnp.int32)[:, None]).astype(
        flat_rows.dtype
    )
    return jnp.dot(selector, flat_rows, preferred_element_type=jnp.float32).astype(flat_rows.dtype)


def project_rows(row_values, w_down):
    columns = lax.all_to_all(row_values, "img", split_axis=1, concat_axis=0, tiled=True)
    return lax.psum_scatter(
        lax.dot_general(
            columns, w_down, (((1,), (1,)), ((), ())), preferred_element_type=jnp.float32
        ).astype(jnp.bfloat16),
        "img",
        scatter_dimension=0,
        tiled=True,
    ).astype(jnp.float32)


def window_backward(query_rows, key_rows, value_rows, grad_rows, window_labels):
    patch_count = query_rows.shape[0]
    patch_width = query_rows.shape[1]
    score_scale = 1.0 / math.sqrt(HEAD_DIM)
    labels = jnp.repeat(window_labels, 4)
    allowed = labels[:, None] == labels[None, :]
    query_heads = query_rows.reshape(patch_count, HEADS, HEAD_DIM)
    key_heads = key_rows.reshape(patch_count, HEADS, HEAD_DIM)
    value_heads = value_rows.reshape(patch_count, HEADS, HEAD_DIM)
    grad_heads = grad_rows.reshape(patch_count, HEADS, HEAD_DIM)
    scores = (
        jnp.einsum("phd,qhd->hpq", query_heads, key_heads, preferred_element_type=jnp.float32)
        * score_scale
    )
    scores = jnp.where(allowed[None, :, :], scores, -jnp.inf)
    peak = jnp.max(scores, axis=2, keepdims=True)
    raw_weights = jnp.exp(scores - peak)
    probs = raw_weights / jnp.sum(raw_weights, axis=2, keepdims=True)
    probs_bf = probs.astype(jnp.bfloat16)
    attended = jnp.einsum("hpq,qhd->phd", probs_bf, value_heads, preferred_element_type=jnp.float32)
    row_delta = jnp.sum(grad_heads.astype(jnp.float32) * attended, axis=2)
    prob_grads = jnp.einsum(
        "phd,qhd->hpq", grad_heads, value_heads, preferred_element_type=jnp.float32
    )
    score_bf = (probs * (prob_grads - jnp.transpose(row_delta)[:, :, None])).astype(jnp.bfloat16)
    grad_query = (
        jnp.einsum("hpq,qhd->phd", score_bf, key_heads, preferred_element_type=jnp.float32)
        * score_scale
    )
    grad_key = (
        jnp.einsum("hpq,phd->qhd", score_bf, query_heads, preferred_element_type=jnp.float32)
        * score_scale
    )
    grad_value = jnp.einsum(
        "hpq,phd->qhd", probs_bf, grad_heads, preferred_element_type=jnp.float32
    )
    return (
        grad_query.reshape(patch_count, patch_width).astype(jnp.bfloat16),
        grad_key.reshape(patch_count, patch_width).astype(jnp.bfloat16),
        grad_value.reshape(patch_count, patch_width).astype(jnp.bfloat16),
    )


def body(llm_grads, token_target, patches, gain, w_down, queries, keys, values, window_ids):
    grad_rows = llm_grads[0]
    targets = token_target[0]
    row_count = grad_rows.shape[0]
    peer_count = lax.axis_size("seq")
    capacity = max(1, 2 * row_count // peer_count)
    packed, slot_labels = pack_rows(grad_rows, targets, peer_count, capacity)
    arrived, arrived_labels = (
        lax.all_to_all(packed, "seq", split_axis=0, concat_axis=0, tiled=True),
        lax.all_to_all(slot_labels, "seq", split_axis=0, concat_axis=0, tiled=True),
    )
    merged = project_rows(unpack_rows(arrived, arrived_labels, row_count), w_down).astype(
        jnp.bfloat16
    )
    patch_width = patches.shape[2]
    patch_grads = merged.reshape(-1, patch_width).astype(jnp.float32)
    inputs = patches[0].astype(jnp.float32)
    inverse_rms = lax.rsqrt(jnp.mean(inputs * inputs, axis=1, keepdims=True) + 1e-06)
    normed = inputs * inverse_rms
    gain_part = jnp.sum(patch_grads * normed, axis=0)
    bias_part = jnp.sum(grad_rows.astype(jnp.float32), axis=0)
    gain_total, bias_total = lax.psum((gain_part, bias_part), ("img", "seq"))
    device_count = lax.axis_size("img") * lax.axis_size("seq")
    gain_grad = gain_total / math.sqrt(device_count * inputs.shape[0])
    bias_grad = bias_total / math.sqrt(device_count * row_count)
    scaled = gain[None, :] * patch_grads
    out_grads = (
        inverse_rms * (scaled - normed * jnp.mean(scaled * normed, axis=1, keepdims=True))
    ).astype(jnp.bfloat16)
    grad_query, grad_key, grad_value = window_backward(
        queries[0], keys[0], values[0], out_grads, window_ids[0, 0]
    )
    return (grad_query[None], grad_key[None], grad_value[None], gain_grad, bias_grad)


def solution(mesh):
    return jax.shard_map(
        body,
        mesh=mesh,
        in_specs=(
            P("img", "seq", None),
            P("img", "seq"),
            P("img", "seq", None),
            P(),
            P(None, "img"),
            P("img", "seq", None),
            P("img", "seq", None),
            P("img", "seq", None),
            P("img", "seq", None),
        ),
        out_specs=(P("img", "seq", None), P("img", "seq", None), P("img", "seq", None), P(), P()),
        check_vma=False,
    )
```

profile of v0, /device:TPU:1, one launch (start us, length us, event | category | flops | bytes accessed | tf_op | source)
XLA Modules:
  0.0 307.9 jit_solution(1589726979734830096)
XLA Ops:
  7.2 0.7 fusion.20
  7.8 0.7 and_select_fusion.1
  8.5 0.2 convert_reduce_fusion.2
  8.7 0.1 select_reduce_fusion
  8.8 0.7 copy.78
  9.5 23.2 %all-to-all-start = ((bf16[64,1,1]{2,1,0:T(2,128)(2,1)}), bf16[64,1,1]{2,1,0:T(2,128)(2,1)S(1)}, u32[]{:S(2)}, u32[]{:S(2)}) async-start(bf16[64,1,1]{2,1,0:T(2,128)(2,1)} %copy.78), calls=%async_computation | async-start | bytes 65536 | tf_op jit(solution)/shard_map/all_to_all | solution.py:108
  32.7 1.6 fusion.1
  34.3 0.5 broadcast.165
  34.8 1.4 reduce.2
  36.2 1.6 reshape.204
  37.8 5.6 %all-to-all-done = bf16[64,1,1]{2,1,0:T(2,128)(2,1)S(1)} async-done(((bf16[64,1,1]{2,1,0:T(2,128)(2,1)}), bf16[64,1,1]{2,1,0:T(2,128)(2,1)S(1)}, u32[]{:S(2)}, u32[]{:S(2)}) %all-to-all-start) | async-done | bytes 160 | tf_op jit(solution)/shard_map/all_to_all | solution.py:108
  43.5 6.5 %all-to-all-start.1 = ((bf16[64,2,4096]{2,1,0:T(2,128)(2,1)}), bf16[64,2,4096]{2,1,0:T(2,128)(2,1)S(1)}, u32[]{:S(2)}, u32[]{:S(2)}) async-start(bf16[64,2,4096]{2,1,0:T(2,128)(2,1)} %reshape.204), calls=%async_computation.1 | async-start | bytes 2097152 | tf_op jit(solution)/shard_map/all_to_all | solution.py:107
  50.0 0.0 reduce-scatter.2.cloned.1.call-start
  50.1 1.2 convert_reduce_fusion.1
  51.3 25.3 %all-to-all-done.1 = bf16[64,2,4096]{2,1,0:T(2,128)(2,1)S(1)} async-done(((bf16[64,2,4096]{2,1,0:T(2,128)(2,1)}), bf16[64,2,4096]{2,1,0:T(2,128)(2,1)S(1)}, u32[]{:S(2)}, u32[]{:S(2)}) %all-to-all-start.1) | async-done | bytes 1048608 | tf_op jit(solution)/shard_map/all_to_all | solution.py:107
  76.6 1.0 reshape.205
  77.6 1.3 convolution_convert_fusion.1
  79.0 28.8 %all_to_all.30 = bf16[32,16,512]{2,0,1:T(8,128)(2,1)S(1)} all-to-all(bf16[32,16,512]{2,0,1:T(8,128)(2,1)S(1)} %bitcast.79), channel_id=1, replica_groups=mesh['img'=16,'seq'=64] {'img'}, dimensions={1} | all-to-all | bytes 1048576 | tf_op jit(solution)/shard_map/all_to_all | solution.py:45
  107.8 7.4 %convolution_convert_fusion.2 = bf16[512,5120]{1,0:T(8,128)(2,1)} fusion(bf16[512,512]{1,0:T(8,128)(2,1)S(1)} %bitcast.86, bf16[5120,512]{1,0:T(8,128)(2,1)} %param.13), kind=kOutput, calls=%fused_computation.4 | convolution fusion | flops 2686976000 | bytes 11010048 | tf_op jit(solution)/shard_map/dot_general | solution.py:47
  115.2 0.0 copy-start
  115.2 0.0 copy-start.6
  115.2 0.0 copy-start.3
  115.2 0.0 copy-start.7
  115.2 0.0 copy-start.4
  115.2 0.0 copy-start.1
  115.2 0.0 reduce-scatter.2.cloned.1.call-update
  115.3 0.9 copy-done
  116.2 0.2 copy.82
  116.3 0.0 copy-done.6
  116.3 0.1 mul.77
  116.4 0.0 copy-done.2
  116.4 0.2 copy.76
  116.6 0.0 copy-done.3
  116.6 0.2 copy.77
  116.8 0.0 copy-done.7
  116.9 0.1 broadcast_in_dim.24
  116.9 0.1 eq.64
  117.0 0.0 copy-done.4
  117.0 0.9 copy.83
  117.9 0.1 fusion.13
  118.1 0.0 copy-done.1
  118.1 0.1 convert_reduce_fusion
  118.2 0.1 broadcast_compare_fusion
  118.3 1.5 fusion.27
  119.8 54.4 %reduce-scatter.2.cloned.1.call-done = bf16[32,5120]{1,0:T(8,128)(2,1)} async-done(((bf16[512,5120]{1,0:T(8,128)(2,1)}), bf16[32,5120]{1,0:T(8,128)(2,1)}) %reduce-scatter.2.cloned.1.call-update) | async-done | bytes 327696 | tf_op jit(solution)/shard_map/reduce_scatter | solution.py:46
  174.2 1.2 reshape.202
  175.4 0.3 multiply_reduce_fusion
  175.7 1.6 reshape.200
  177.3 0.5 copy.81
  177.7 0.0 copy-start.8
  177.7 0.2 multiply_convert_fusion
  178.0 1.7 fusion.10
  179.7 0.0 copy-done.5
  179.7 0.0 copy-done.8
  179.7 0.4 fusion.6
  180.1 0.5 fusion.8
  180.6 0.3 fusion.9
  180.9 0.5 convolution_convert_fusion.3
  181.4 0.9 copy.90
  182.3 0.9 copy.89
  183.2 0.9 copy.91
  184.2 115.7 %all-reduce = (f32[1280]{0:T(1024)S(1)}, f32[8192]{0:T(1024)S(1)}) all-reduce(f32[1280]{0:T(1024)S(1)} %get-tuple-element.30, f32[8192]{0:T(1024)S(1)} %convert_reduce_fusion), channel_id=1, replica_groups=mesh['img'=16,'seq'=64] {'img','seq'}, use_global_device_ids=true, to_apply=%region_9.10 | all-reduce | flops 9472 | bytes 75776 | tf_op jit(solution)/shard_map/psum | solution.py:120
  299.8 0.6 broadcast_multiply_fusion
  300.4 0.6 broadcast_multiply_fusion.1
  (7 shorter events, 0.1 us)
Async XLA Ops:
  9.5 33.9 %all-to-all-start = ((bf16[64,1,1]{2,1,0:T(2,128)(2,1)}), bf16[64,1,1]{2,1,0:T(2,128)(2,1)S(1)}, u32[]{:S(2)}, u32[]{:S(2)}) async-start(bf16[64,1,1]{2,1,0:T(2,128)(2,1)} %copy.78), calls=%async_computation | async-start | bytes 65536 | tf_op jit(solution)/shard_map/all_to_all | solution.py:108
  43.5 33.1 %all-to-all-start.1 = ((bf16[64,2,4096]{2,1,0:T(2,128)(2,1)}), bf16[64,2,4096]{2,1,0:T(2,128)(2,1)S(1)}, u32[]{:S(2)}, u32[]{:S(2)}) async-start(bf16[64,2,4096]{2,1,0:T(2,128)(2,1)} %reshape.204), calls=%async_computation.1 | async-start | bytes 2097152 | tf_op jit(solution)/shard_map/all_to_all | solution.py:107
  50.0 124.2 %reduce-scatter.2.cloned.1.call-start = ((), (), s32[]{:S(2)}) async-start(), calls=%async_computation.4 | async-start | bytes 5570560 | tf_op jit(solution)/shard_map/reduce_scatter | solution.py:46
  115.2 1.0 copy-start
  115.2 1.1 copy-start.6
  115.2 1.2 copy-start.2
  115.2 1.4 copy-start.3
  115.2 1.7 copy-start.7
  115.2 1.8 copy-start.4
  115.2 2.9 copy-start.1
  175.7 4.0 %copy-start.5 = (bf16[1,128,1280]{1,2,0:T(8,128)(2,1)S(1)}, bf16[1,128,1280]{1,2,0:T(8,128)(2,1)}, u32[]{:S(2)}) copy-start(bf16[1,128,1280]{1,2,0:T(8,128)(2,1)} %copy.83) | copy-start | bytes 983044
  177.7 2.0 copy-start.8
Sparse Core Ops, SparseCore 0:
  115.4 58.8 reduce-scatter.1
where the time goes:
time: 308 us
  blocking collectives  144 us (47%)
  waiting for transfers between devices  85.3 us (28%)
  starting transfers between devices  29.7 us (10%)
  matrix products  15.2 us (5%)
  between operations  14.3 us (5%)
  local copies, waits for them, and re-layouts  12.5 us (4%)
  other arithmetic  6.41 us (2%)
    psum x1, blocking collectives, body(): gain_total, bias_total = lax.psum((gain_part, bias_part), ('img', 'seq'))  116 us
    reduce_scatter x1, waiting for transfers between devices, project_rows(): lax.psum_scatter(lax.dot_general(columns, w_down, (((1,), (1,)), ((), ())...  54.4 us
    all_to_all x1, blocking collectives, project_rows(): lax.all_to_all(row_values, 'img', split_axis=1, concat_axis=0, tiled=True)  28.8 us
    all_to_all x1, waiting for transfers between devices, body(): lax.all_to_all(packed, 'seq', split_axis=0, concat_axis=0, tiled=True)  25.3 us
    all_to_all x1, starting transfers between devices, body(): lax.all_to_all(slot_labels, 'seq', split_axis=0, concat_axis=0, tiled=True)  23.2 us
    unnamed x26, local copies, waits for them, and re-layouts  7.62 us
    dot_general x1, matrix products, project_rows(): lax.dot_general(columns, w_down, (((1,), (1,)), ((), ())), preferred_elem...  7.38 us
    all_to_all x1, starting transfers between devices, body(): lax.all_to_all(packed, 'seq', split_axis=0, concat_axis=0, tiled=True)  6.53 us
  transfers between devices with their start and end apart: 3, of which 3 were waited for; matrix products, arithmetic and copies ran while one was open for 3% of the time, Pallas kernels for 0%

commit v1 on v0

--- a/solution.py
+++ b/solution.py
@@ -1,8 +1,11 @@
+import functools
 import math
 
 import jax
 import jax.numpy as jnp
 from jax import lax
+from jax.experimental import pallas as pl
+from jax.experimental.pallas import tpu as pltpu
 from jax.sharding import PartitionSpec as P
 
 HEADS = 16
@@ -18,39 +21,153 @@
 def pack_rows(row_values, targets, peer_count, capacity):
     row_count = row_values.shape[0]
     destination = targets // row_count
-    local_row = targets % row_count
+    local_row = (targets % row_count).astype(jnp.float32).astype(row_values.dtype)
     slot_index = destination * capacity + earlier_equal(
         destination, jnp.arange(row_count, dtype=jnp.int32)
     )
     matches = slot_index[None, :] == jnp.arange(peer_count * capacity, dtype=jnp.int32)[:, None]
     selector = matches.astype(row_values.dtype)
-    packed = jnp.dot(selector, row_values, preferred_element_type=jnp.float32).astype(
-        row_values.dtype
-    )
-    slot_rows = jnp.sum(jnp.where(matches, local_row[None, :] + 1, 0), axis=1) - 1
-    slot_labels = slot_rows.astype(jnp.float32).astype(jnp.bfloat16).reshape(peer_count, capacity)
-    return (packed.reshape(peer_count, capacity, row_values.shape[1]), slot_labels)
-
-
-def unpack_rows(received, slot_labels, row_count):
-    flat_rows = received.reshape(-1, received.shape[2])
-    flat_labels = slot_labels.reshape(-1).astype(jnp.float32).astype(jnp.int32)
-    selector = (flat_labels[None, :] == jnp.arange(row_count, dtype=jnp.int32)[:, None]).astype(
-        flat_rows.dtype
-    )
-    return jnp.dot(selector, flat_rows, preferred_element_type=jnp.float32).astype(flat_rows.dtype)
+    labelled = jnp.concatenate(
+        [row_values, jnp.broadcast_to(local_row[:, None] + 1, (row_count, 128))], axis=1
+    )
+    return jnp.dot(selector, labelled, preferred_element_type=jnp.float32).astype(row_values.dtype)
+
+
+def unpack_rows(received, row_count):
+    width = received.shape[1] - 128
+    labels = received[:, width].astype(jnp.float32).astype(jnp.int32) - 1
+    selector = (labels[None, :] == jnp.arange(row_count, dtype=jnp.int32)[:, None]).astype(
+        received.dtype
+    )
+    return jnp.dot(
+        selector, received[:, :width], preferred_element_type=jnp.float32
+    ).astype(received.dtype)
 
 
 def project_rows(row_values, w_down):
     columns = lax.all_to_all(row_values, "img", split_axis=1, concat_axis=0, tiled=True)
-    return lax.psum_scatter(
+    bias_part = jnp.sum(columns.astype(jnp.float32), axis=0)
+    products = lax.psum_scatter(
         lax.dot_general(
             columns, w_down, (((1,), (1,)), ((), ())), preferred_element_type=jnp.float32
         ).astype(jnp.bfloat16),
         "img",
         scatter_dimension=0,
         tiled=True,
-    ).astype(jnp.float32)
+    )
+    return products, bias_part
+
+
+def ring_sum_kernel(
+    n_img, n_side, gain_rows, terms, gain_out, bias_out, side_a, side_b, across, send_sem, recv_sem
+):
+    img = lax.axis_index("img")
+    seq = lax.axis_index("seq")
+    high = seq // n_side
+    low = lax.rem(seq, n_side)
+
+    def along_a(at):
+        return (img, at * n_side + low)
+
+    def along_b(at):
+        return (img, high * n_side + at)
+
+    def along_img(at):
+        return (at, seq)
+
+    stages = (
+        (side_a, n_side, high, along_a),
+        (side_b, n_side, low, along_b),
+        (across, n_img, img, along_img),
+    )
+    barrier = pltpu.get_barrier_semaphore()
+    for _, size, own, peer in stages:
+        for step in range(1, size):
+            pl.semaphore_signal(
+                barrier,
+                inc=1,
+                device_id=peer(lax.rem(own + step, size)),
+                device_id_type=pl.DeviceIdType.MESH,
+            )
+    pl.semaphore_wait(barrier, 2 * (n_side - 1) + n_img - 1)
+
+    first = 0
+    held = terms[...]
+    for slots, size, own, peer in stages:
+        slots[own] = held
+        copies = []
+        for step in range(1, size):
+            target = lax.rem(own + step, size)
+            copy = pltpu.make_async_remote_copy(
+                src_ref=slots.at[own],
+                dst_ref=slots.at[own],
+                send_sem=send_sem.at[first + step],
+                recv_sem=recv_sem.at[first + step],
+                device_id=peer(target),
+                device_id_type=pl.DeviceIdType.MESH,
+            )
+            copy.start()
+            copies.append(copy)
+        for step in range(1, size):
+            source = lax.rem(own + size - step, size)
+            pltpu.make_async_remote_copy(
+                src_ref=slots.at[source],
+                dst_ref=slots.at[source],
+                send_sem=send_sem.at[first + step],
+                recv_sem=recv_sem.at[first + step],
+                device_id=peer(source),
+                device_id_type=pl.DeviceIdType.MESH,
+            ).wait_recv()
+        for copy in copies:
+            copy.wait_send()
+        first += size
+        if slots is across:
+            total = slots[0][:gain_rows]
+            for at in range(1, size):
+                total += slots[at][:gain_rows]
+            gain_out[...] = total
+            bias_out[...] = slots[:, gain_rows:, :]
+        else:
+            held = slots[0]
+            for at in range(1, size):
+                held += slots[at]
+
+
+def sum_terms(gain_part, bias_part):
+    n_img = lax.axis_size("img")
+    n_seq = lax.axis_size("seq")
+    n_side = math.isqrt(n_seq)
+    gain_rows = -(-gain_part.shape[0] // 1024) * 8
+    bias_rows = -(-bias_part.shape[0] // 1024) * 8
+    gain_padded = jnp.pad(gain_part, (0, gain_rows * 128 - gain_part.shape[0]))
+    bias_padded = jnp.pad(bias_part, (0, bias_rows * 128 - bias_part.shape[0]))
+    rows = gain_rows + bias_rows
+    terms = jnp.concatenate([gain_padded, bias_padded]).reshape(rows, 128)
+    copies = n_img + 2 * n_side
+    gain_total, bias_total = pl.pallas_call(
+        functools.partial(ring_sum_kernel, n_img, n_side, gain_rows),
+        out_shape=(
+            jax.ShapeDtypeStruct((gain_rows, 128), jnp.float32),
+            jax.ShapeDtypeStruct((n_img, bias_rows, 128), jnp.float32),
+        ),
+        in_specs=[pl.BlockSpec(memory_space=pltpu.VMEM)],
+        out_specs=(
+            pl.BlockSpec(memory_space=pltpu.VMEM),
+            pl.BlockSpec(memory_space=pltpu.VMEM),
+        ),
+        scratch_shapes=[
+            pltpu.VMEM((n_side, rows, 128), jnp.float32),
+            pltpu.VMEM((n_side, rows, 128), jnp.float32),
+            pltpu.VMEM((n_img, rows, 128), jnp.float32),
+            pltpu.SemaphoreType.DMA((copies,)),
+            pltpu.SemaphoreType.DMA((copies,)),
+        ],
+        compiler_params=pltpu.CompilerParams(collective_id=0, has_side_effects=True),
+        name="sum_terms",
+    )(terms)
+    gain_total = gain_total.reshape(-1)[: gain_part.shape[0]]
+    bias_total = bias_total.reshape(n_img, -1)[:, : bias_part.shape[0]].reshape(-1)
+    return gain_total, bias_total
 
 
 def window_backward(query_rows, key_rows, value_rows, grad_rows, window_labels):
@@ -102,22 +219,17 @@
     row_count = grad_rows.shape[0]
     peer_count = lax.axis_size("seq")
     capacity = max(1, 2 * row_count // peer_count)
-    packed, slot_labels = pack_rows(grad_rows, targets, peer_count, capacity)
-    arrived, arrived_labels = (
-        lax.all_to_all(packed, "seq", split_axis=0, concat_axis=0, tiled=True),
-        lax.all_to_all(slot_labels, "seq", split_axis=0, concat_axis=0, tiled=True),
-    )
-    merged = project_rows(unpack_rows(arrived, arrived_labels, row_count), w_down).astype(
-        jnp.bfloat16
-    )
+    products, bias_part = project_rows(grad_rows, w_down)
+    packed = pack_rows(products, targets, peer_count, capacity)
+    arrived = lax.all_to_all(packed, "seq", split_axis=0, concat_axis=0, tiled=True)
+    merged = unpack_rows(arrived, row_count)
     patch_width = patches.shape[2]
     patch_grads = merged.reshape(-1, patch_width).astype(jnp.float32)
     inputs = patches[0].astype(jnp.float32)
     inverse_rms = lax.rsqrt(jnp.mean(inputs * inputs, axis=1, keepdims=True) + 1e-06)
     normed = inputs * inverse_rms
     gain_part = jnp.sum(patch_grads * normed, axis=0)
-    bias_part = jnp.sum(grad_rows.astype(jnp.float32), axis=0)
-    gain_total, bias_total = lax.psum((gain_part, bias_part), ("img", "seq"))
+    gain_total, bias_total = sum_terms(gain_part, bias_part)
     device_count = lax.axis_size("img") * lax.axis_size("seq")
     gain_grad = gain_total / math.sqrt(device_count * inputs.shape[0])
     bias_grad = bias_total / math.sqrt(device_count * row_count)

time: 308 us -> 201 us (0.65)
  blocking collectives: 144 us -> 33.9 us
  Pallas kernels: 0 us -> 31.7 us
  starting transfers between devices: 29.7 us -> 11.2 us
  waiting for transfers between devices: 85.3 us -> 79 us
    psum x1 -> x0, blocking collectives: 116 us -> none  [body(): gain_total, bias_total = lax.psum((gain_part, bias_part), ('img', 'seq'))]
    pallas_call x0 -> x1, Pallas kernels: none -> 31.7 us  [sum_terms(): pl.pallas_call(functools.partial(ring_sum_kernel, n_img, n_side, gain_row...]
    all_to_all x1 -> x0, starting transfers between devices: 23.2 us -> none  [body(): lax.all_to_all(slot_labels, 'seq', split_axis=0, concat_axis=0, tiled=True)]
    all_to_all x1, waiting for transfers between devices: 25.3 us -> 12.4 us  [body(): lax.all_to_all(packed, 'seq', split_axis=0, concat_axis=0, tiled=True)]
    reduce_scatter x1, waiting for transfers between devices: 54.4 us -> 66.6 us  [project_rows(): lax.psum_scatter(lax.dot_general(columns, w_down, (((1,), (1,)), ((), ())...]
    all_to_all x1 -> x0, waiting for transfers between devices: 5.62 us -> none  [body(): lax.all_to_all(slot_labels, 'seq', split_axis=0, concat_axis=0, tiled=True)]
    all_to_all x1, blocking collectives: 28.8 us -> 33.9 us  [project_rows(): lax.all_to_all(row_values, 'img', split_axis=1, concat_axis=0, tiled=True)]
    all_to_all x1, starting transfers between devices: 6.53 us -> 11.2 us  [body(): lax.all_to_all(packed, 'seq', split_axis=0, concat_axis=0, tiled=True)]
  transfers between devices with their start and end apart: 3 -> 2, of which waited for: 3 -> 2; matrix products, arithmetic and copies ran while one was open for 3% -> 2% of each run, Pallas kernels for 0% -> 0%
where the time goes in v1:
time: 201 us
  waiting for transfers between devices  79 us (39%)
  blocking collectives  33.9 us (17%)
  Pallas kernels  31.7 us (16%)
  between operations  14.3 us (7%)
  matrix products  13.6 us (7%)
  local copies, waits for them, and re-layouts  12.4 us (6%)
  starting transfers between devices  11.2 us (6%)
  other arithmetic  4.19 us (2%)
    reduce_scatter x1, waiting for transfers between devices, project_rows(): lax.psum_scatter(lax.dot_general(columns, w_down, (((1,), (1,)), ((), ())...  66.6 us
    all_to_all x1, blocking collectives, project_rows(): lax.all_to_all(row_values, 'img', split_axis=1, concat_axis=0, tiled=True)  33.9 us
    pallas_call x1, Pallas kernels, sum_terms(): pl.pallas_call(functools.partial(ring_sum_kernel, n_img, n_side, gain_row...  31.7 us
    all_to_all x1, waiting for transfers between devices, body(): lax.all_to_all(packed, 'seq', split_axis=0, concat_axis=0, tiled=True)  12.4 us
    all_to_all x1, starting transfers between devices, body(): lax.all_to_all(packed, 'seq', split_axis=0, concat_axis=0, tiled=True)  11.2 us
    unnamed x38, local copies, waits for them, and re-layouts  9.97 us
    dot_general x1, matrix products, project_rows(): lax.dot_general(columns, w_down, (((1,), (1,)), ((), ())), preferred_elem...  7.15 us
  transfers between devices with their start and end apart: 2, of which 2 were waited for; matrix products, arithmetic and copies ran while one was open for 2% of the time, Pallas kernels for 0%

profile of v1, /device:TPU:1, one launch (start us, length us, event | category | flops | bytes accessed | tf_op | source)
XLA Modules:
  0.0 200.5 jit_solution(11647150521167053798)
XLA Ops:
  7.2 0.0 reduce-scatter.2.cloned.1.call-start
  7.2 1.2 copy.108
  8.4 0.3 copy.89
  8.7 33.9 %all_to_all.31 = bf16[32,16,512]{2,0,1:T(8,128)(2,1)S(1)} all-to-all(bf16[32,16,512]{2,0,1:T(8,128)(2,1)S(1)} %copy.89), channel_id=1, replica_groups=mesh['img'=16,'seq'=64] {'img'}, dimensions={1} | all-to-all | bytes 1048576 | tf_op jit(solution)/shard_map/all_to_all | solution.py:48
  42.7 7.1 %convolution_convert_fusion = bf16[512,5120]{1,0:T(8,128)(2,1)} fusion(bf16[512,512]{1,0:T(8,128)(2,1)S(1)} %bitcast.91, bf16[5120,512]{1,0:T(8,128)(2,1)} %param.13), kind=kOutput, calls=%fused_computation.1 | convolution fusion | flops 2686976000 | bytes 11010048 | tf_op jit(solution)/shard_map/dot_general | solution.py:51
  49.8 0.0 copy-start.6
  49.8 0.0 copy-start.10
  49.8 0.0 copy-start.7
  49.9 0.0 reduce-scatter.2.cloned.1.call-update
  49.9 0.6 copy-done.11
  50.5 0.2 convert_reduce_fusion.1
  50.7 66.6 %reduce-scatter.2.cloned.1.call-done = bf16[32,5120]{1,0:T(8,128)(2,1)} async-done(((bf16[512,5120]{1,0:T(8,128)(2,1)}), bf16[32,5120]{1,0:T(8,128)(2,1)}) %reduce-scatter.2.cloned.1.call-update) | async-done | bytes 327696 | tf_op jit(solution)/shard_map/reduce_scatter | solution.py:50
  117.3 0.1 broadcast_in_dim.15
  117.4 1.3 fusion.1
  118.7 0.5 broadcast.201
  119.2 1.1 reduce.3
  120.3 1.6 reshape.218
  121.8 11.2 %all-to-all-start.1 = ((bf16[64,2,2624]{2,1,0:T(2,128)(2,1)}), bf16[64,2,2624]{2,1,0:T(2,128)(2,1)S(1)}, u32[]{:S(2)}, u32[]{:S(2)}) async-start(bf16[64,2,2624]{2,1,0:T(2,128)(2,1)} %reshape.218), calls=%async_computation.2 | async-start | bytes 1376256 | tf_op jit(solution)/shard_map/all_to_all | solution.py:224
  133.0 0.0 copy-done
  133.1 0.2 copy.92
  133.2 0.0 copy-done.9
  133.2 0.1 mul.77
  133.3 0.0 copy-done.5
  133.3 0.2 copy.87
  133.5 0.0 copy-done.6
  133.5 0.0 copy-start.3
  133.5 0.2 copy.88
  133.8 0.0 copy-start.1
  133.8 0.0 copy-done.10
  133.8 0.1 broadcast_in_dim.12
  133.9 0.1 eq.64
  134.0 0.0 copy-done.7
  134.0 0.9 copy.93
  134.9 0.1 fusion.13
  135.0 0.1 broadcast_compare_fusion
  135.1 1.5 fusion.33
  136.6 0.1 convert_reduce_fusion
  136.7 12.4 %all-to-all-done.1 = bf16[64,2,2624]{2,1,0:T(2,128)(2,1)S(1)} async-done(((bf16[64,2,2624]{2,1,0:T(2,128)(2,1)}), bf16[64,2,2624]{2,1,0:T(2,128)(2,1)S(1)}, u32[]{:S(2)}, u32[]{:S(2)}) %all-to-all-start.1) | async-done | bytes 671776 | tf_op jit(solution)/shard_map/all_to_all | solution.py:224
  149.1 1.0 reshape.219
  150.1 0.1 copy.113
  150.2 0.1 add_reduce_fusion
  150.3 0.2 fusion.2
  150.5 0.2 reshape.216
  150.7 0.5 reshape.214
  151.3 0.3 multiply_reduce_fusion
  151.6 0.4 copy.91
  152.0 0.0 copy-start.12
  152.0 0.0 copy-start.4
  152.0 0.2 multiply_convert_fusion
  152.3 0.0 copy-start.2
  152.3 1.8 fusion.11
  154.1 0.4 fusion.7
  154.5 0.5 fusion.9
  155.0 0.0 copy-done.2
  155.0 0.3 fusion.10
  155.3 0.5 convolution_convert_fusion.3
  155.8 0.9 copy.100
  156.7 0.9 copy.99
  157.6 0.9 copy.101
  158.6 0.6 fusion.21.terms
  159.2 31.7 %sum_terms.1 = (f32[16,128]{1,0:T(8,128)}, f32[16,8,128]{2,1,0:T(8,128)}) custom-call(f32[24,128]{1,0:T(8,128)} %fusion.21.terms), custom_call_target="tpu_custom_call" | custom-call | tf_op jit(solution)/shard_map/sum_terms/pallas_call | solution.py:147
  190.9 0.9 copy.114
  191.7 0.6 copy.110
  192.4 1.3 multiply_bitcast_fusion
  (17 shorter events, 0.1 us)
Async XLA Ops:
  7.2 110.2 %reduce-scatter.2.cloned.1.call-start = ((), (), s32[]{:S(2)}) async-start(), calls=%async_computation.3 | async-start | bytes 5570560 | tf_op jit(solution)/shard_map/reduce_scatter | solution.py:50
  49.8 0.7 copy-start.11
  49.8 83.2 %copy-start = (bf16[1,128,1280]{2,1,0:T(8,128)(2,1)S(1)}, bf16[1,128,1280]{2,1,0:T(8,128)(2,1)}, u32[]{:S(2)}) copy-start(bf16[1,128,1280]{2,1,0:T(8,128)(2,1)} %param.11) | copy-start | bytes 983044
  49.8 83.4 %copy-start.9 = (f32[1280]{0:T(1024)S(1)}, f32[1280]{0:T(1024)}, u32[]{:S(2)}) copy-start(f32[1280]{0:T(1024)} %param.12) | copy-start | bytes 15364
  49.8 83.5 %copy-start.5 = (bf16[1,128,1280]{2,1,0:T(8,128)(2,1)S(1)}, bf16[1,128,1280]{2,1,0:T(8,128)(2,1)}, u32[]{:S(2)}) copy-start(bf16[1,128,1280]{2,1,0:T(8,128)(2,1)} %param.14) | copy-start | bytes 983044
  49.8 83.7 %copy-start.6 = (bf16[1,128,1280]{2,1,0:T(8,128)(2,1)S(1)}, bf16[1,128,1280]{2,1,0:T(8,128)(2,1)}, u32[]{:S(2)}) copy-start(bf16[1,128,1280]{2,1,0:T(8,128)(2,1)} %param.15) | copy-start | bytes 983044
  49.8 83.9 %copy-start.10 = (s32[1,1,32]{2,1,0:T(1,128)S(1)}, s32[1,1,32]{2,1,0:T(1,128)}, u32[]{:S(2)}) copy-start(s32[1,1,32]{2,1,0:T(1,128)} %param.17) | copy-start | bytes 388
  49.8 84.1 %copy-start.7 = (bf16[1,128,1280]{2,1,0:T(8,128)(2,1)S(1)}, bf16[1,128,1280]{2,1,0:T(8,128)(2,1)}, u32[]{:S(2)}) copy-start(bf16[1,128,1280]{2,1,0:T(8,128)(2,1)} %param.16) | copy-start | bytes 983044
  121.8 27.3 %all-to-all-start.1 = ((bf16[64,2,2624]{2,1,0:T(2,128)(2,1)}), bf16[64,2,2624]{2,1,0:T(2,128)(2,1)S(1)}, u32[]{:S(2)}, u32[]{:S(2)}) async-start(bf16[64,2,2624]{2,1,0:T(2,128)(2,1)} %reshape.218), calls=%async_computation.2 | async-start | bytes 1376256 | tf_op jit(solution)/shard_map/all_to_all | solution.py:224
  133.5 3.2 %copy-start.3 = (bf16[1,128,1280]{1,2,0:T(8,128)(2,1)}, bf16[1,128,1280]{1,2,0:T(8,128)(2,1)S(1)}, u32[]{:S(2)}) copy-start(bf16[1,128,1280]{1,2,0:T(8,128)(2,1)S(1)} %copy.87) | copy-start | bytes 983044
  133.8 3.0 %copy-start.1 = (bf16[1,128,1280]{1,2,0:T(8,128)(2,1)}, bf16[1,128,1280]{1,2,0:T(8,128)(2,1)S(1)}, u32[]{:S(2)}) copy-start(bf16[1,128,1280]{1,2,0:T(8,128)(2,1)S(1)} %copy.88) | copy-start | bytes 983044
  151.5 2.6 %copy-start.8 = (bf16[1,128,1280]{1,2,0:T(8,128)(2,1)S(1)}, bf16[1,128,1280]{1,2,0:T(8,128)(2,1)}, u32[]{:S(2)}) copy-start(bf16[1,128,1280]{1,2,0:T(8,128)(2,1)} %copy.93) | copy-start | bytes 983044
  152.0 2.1 %copy-start.12 = (f32[16,128,128]{1,2,0:T(8,128)S(1)}, f32[16,128,128]{1,2,0:T(8,128)}, u32[]{:S(2)}) copy-start(f32[16,128,128]{1,2,0:T(8,128)} %get-tuple-element.42) | copy-start | bytes 3145732
  152.0 2.5 %copy-start.4 = (bf16[1,128,1280]{1,2,0:T(8,128)(2,1)S(1)}, bf16[1,128,1280]{1,2,0:T(8,128)(2,1)}, u32[]{:S(2)}) copy-start(bf16[1,128,1280]{1,2,0:T(8,128)(2,1)} %copy-done.3) | copy-start | bytes 983044
  152.3 2.7 %copy-start.2 = (bf16[1,128,1280]{1,2,0:T(8,128)(2,1)S(1)}, bf16[1,128,1280]{1,2,0:T(8,128)(2,1)}, u32[]{:S(2)}) copy-start(bf16[1,128,1280]{1,2,0:T(8,128)(2,1)} %copy-done.1) | copy-start | bytes 983044
Sparse Core Ops, SparseCore 0:
  50.0 67.2 reduce-scatter.1

commit v2 on v1

--- a/solution.py
+++ b/solution.py
@@ -44,18 +44,324 @@
     ).astype(received.dtype)
 
 
+CORES = 2
+CHUNKS = 5
+MESH = pl.DeviceIdType.MESH
+
+
+def project_kernel(
+    n_y,
+    grads,
+    w_down,
+    products,
+    bias_part,
+    weights,
+    columns,
+    parts,
+    half_out,
+    half_in,
+    full_out,
+    full_in,
+    summed,
+    swapped,
+    weight_sem,
+    column_send,
+    column_recv,
+    relay_send,
+    relay_recv,
+    ring_send,
+    ring_recv,
+    swap_send,
+    swap_recv,
+):
+    img = lax.axis_index("img")
+    seq = lax.axis_index("seq")
+    y = img // CORES
+    core = lax.rem(img, CORES)
+    other = 1 - core
+    hops = n_y // 2
+    rows, chip_cols = columns.shape[1], columns.shape[2]
+    block = chip_cols // CORES
+    half = weights.shape[1]
+    width = half // CHUNKS
+    side = width // 2
+    chip_rows = CORES * rows
+
+    def at_chip(there, which):
+        return (there * CORES + which, seq)
+
+    twin = at_chip(y, other)
+
+    barrier = pltpu.get_barrier_semaphore()
+    pl.semaphore_signal(barrier, inc=1, device_id=twin, device_id_type=MESH)
+    for step in range(1, n_y):
+        pl.semaphore_signal(
+            barrier,
+            inc=1,
+            device_id=at_chip(lax.rem(y + step, n_y), core),
+            device_id_type=MESH,
+        )
+    pl.semaphore_wait(barrier, n_y)
+
+    def column_copy(step):
+        target = lax.rem(y + step, n_y)
+        start = pl.multiple_of(target * chip_cols, chip_cols)
+        return pltpu.make_async_remote_copy(
+            src_ref=grads.at[:, pl.ds(start, chip_cols)],
+            dst_ref=columns.at[y * CORES + core],
+            send_sem=column_send.at[step],
+            recv_sem=column_recv.at[step],
+            device_id=at_chip(target, core),
+            device_id_type=MESH,
+        )
+
+    def column_arrival(step):
+        source = lax.rem(y + n_y - step, n_y)
+        return pltpu.make_async_remote_copy(
+            src_ref=columns.at[source * CORES + core],
+            dst_ref=columns.at[source * CORES + core],
+            send_sem=column_send.at[step],
+            recv_sem=column_recv.at[step],
+            device_id=at_chip(source, core),
+            device_id_type=MESH,
+        )
+
+    def relay_copy(source):
+        slot = source * CORES + core
+        return pltpu.make_async_remote_copy(
+            src_ref=columns.at[slot],
+            dst_ref=columns.at[slot],
+            send_sem=relay_send.at[source],
+            recv_sem=relay_recv.at[source],
+            device_id=twin,
+            device_id_type=MESH,
+        )
+
+    def relay_arrival(source):
+        slot = source * CORES + other
+        return pltpu.make_async_remote_copy(
+            src_ref=columns.at[slot],
+            dst_ref=columns.at[slot],
+            send_sem=relay_send.at[source],
+            recv_sem=relay_recv.at[source],
+            device_id=twin,
+            device_id_type=MESH,
+        )
+
+    outward = [step for near in range(1, hops + 1) for step in (near, n_y - near)]
+    outward = sorted(set(outward), key=lambda step: (-min(step, n_y - step), step))
+    for step in outward:
+        column_copy(step).start()
+    weight_away = pltpu.make_async_remote_copy(
+        src_ref=w_down.at[pl.ds(pl.multiple_of(other * half, half), half), :],
+        dst_ref=weights.at[core],
+        send_sem=weight_sem.at[0],
+        recv_sem=weight_sem.at[1],
+        device_id=twin,
+        device_id_type=MESH,
+    )
+    weight_away.start()
+    weight_here = pltpu.make_async_copy(
+        w_down.at[pl.ds(pl.multiple_of(core * half, half), half), :],
+        weights.at[core],
+        weight_sem.at[2],
+    )
+    weight_here.start()
+    own_start = pl.multiple_of(y * chip_cols, chip_cols)
+    own_columns = pltpu.make_async_copy(
+        grads.at[:, pl.ds(own_start, chip_cols)],
+        columns.at[y * CORES + core],
+        weight_sem.at[3],
+    )
+    own_columns.start()
+    own_columns.wait()
+    relay_copy(y).start()
+    for step in reversed(outward):
+        column_arrival(step).wait_recv()
+        relay_copy(lax.rem(y + n_y - step, n_y)).start()
+    for source in range(n_y):
+        relay_arrival(source).wait_recv()
+    weight_here.wait()
+    pltpu.make_async_remote_copy(
+        src_ref=weights.at[other],
+        dst_ref=weights.at[other],
+        send_sem=weight_sem.at[0],
+        recv_sem=weight_sem.at[1],
+        device_id=twin,
+        device_id_type=MESH,
+    ).wait_recv()
+
+    def half_copy(way, n):
+        target = lax.rem(y + (1 if way == 0 else n_y - 1), n_y)
+        return pltpu.make_async_remote_copy(
+            src_ref=half_out.at[way, n],
+            dst_ref=half_in.at[way, n],
+            send_sem=ring_send.at[way, 0, n],
+            recv_sem=ring_recv.at[way, 0, n],
+            device_id=at_chip(target, core),
+            device_id_type=MESH,
+        )
+
+    def full_copy(way, step, n):
+        target = lax.rem(y + (1 if way == 0 else n_y - 1), n_y)
+        return pltpu.make_async_remote_copy(
+            src_ref=full_out.at[way, step - 1, n],
+            dst_ref=full_in.at[way, step - 1, n],
+            send_sem=ring_send.at[way, step, n],
+            recv_sem=ring_recv.at[way, step, n],
+            device_id=at_chip(target, core),
+            device_id_type=MESH,
+        )
+
+    def swap_copy(n):
+        return pltpu.make_async_remote_copy(
+            src_ref=summed.at[n, other],
+            dst_ref=swapped.at[n],
+            send_sem=swap_send.at[n],
+            recv_sem=swap_recv.at[n],
+            device_id=twin,
+            device_id_type=MESH,
+        )
+
+    def chip_block(there):
+        return pl.ds(pl.multiple_of(there * chip_rows, chip_rows), chip_rows)
+
+    over_last = (((1,), (1,)), ((), ()))
+
+    def multiply(n, carry):
+        own = pl.ds(pl.multiple_of(n * width, width), width)
+        total = None
+        for which in range(CORES):
+            term = lax.dot_general(
+                columns[:, :, which * block : (which + 1) * block].reshape(-1, block),
+                weights[which, own, :],
+                over_last,
+                preferred_element_type=jnp.float32,
+            )
+            total = term if total is None else total + term
+        parts[n] = total
+        far = parts[n, chip_block(lax.rem(y + hops, n_y)), :]
+        half_out[0, n] = far[:, :side].astype(jnp.bfloat16)
+        half_out[1, n] = far[:, side:].astype(jnp.bfloat16)
+        half_copy(0, n).start()
+        half_copy(1, n).start()
+        return carry
+
+    lax.fori_loop(0, CHUNKS, multiply, 0)
+    bias_part[...] = jnp.sum(
+        columns[...].reshape(-1, chip_cols).astype(jnp.float32), axis=0, keepdims=True
+    )
+
+    for step in range(1, hops):
+
+        def pass_on(n, carry):
+            for way in range(2):
+                distance = hops - step
+                there = lax.rem(y + (distance if way == 0 else n_y - distance), n_y)
+                mine = parts[n, chip_block(there), :]
+                if step == 1:
+                    half_copy(way, n).wait_recv()
+                    arrived = half_in[way, n].astype(jnp.float32)
+                    low, high = mine[:, :side], mine[:, side:]
+                    if way == 0:
+                        low = low + arrived
+                    else:
+                        high = high + arrived
+                    full_out[way, 0, n, :, :side] = low.astype(jnp.bfloat16)
+                    full_out[way, 0, n, :, side:] = high.astype(jnp.bfloat16)
+                else:
+                    full_copy(way, step - 1, n).wait_recv()
+                    arrived = full_in[way, step - 2, n].astype(jnp.float32)
+                    full_out[way, step - 1, n] = (mine + arrived).astype(jnp.bfloat16)
+                full_copy(way, step, n).start()
+            return carry
+
+        lax.fori_loop(0, CHUNKS, pass_on, 0)
+
+    def finish(n, carry):
+        total = parts[n, chip_block(y), :]
+        for way in range(2):
+            full_copy(way, hops - 1, n).wait_recv()
+            total = total + full_in[way, hops - 2, n].astype(jnp.float32)
+        total = total.astype(jnp.bfloat16)
+        for which in range(CORES):
+            summed[n, which] = total[which * rows : (which + 1) * rows]
+        swap_copy(n).start()
+        at = pl.multiple_of(core * half + n * width, width)
+        products[:, pl.ds(at, width)] = summed[n, core]
+        return carry
+
+    lax.fori_loop(0, CHUNKS, finish, 0)
+
+    def collect(n, carry):
+        swap_copy(n).wait_recv()
+        at = pl.multiple_of(other * half + n * width, width)
+        products[:, pl.ds(at, width)] = swapped[n]
+        for way in range(2):
+            half_copy(way, n).wait_send()
+            for step in range(1, hops):
+                full_copy(way, step, n).wait_send()
+        swap_copy(n).wait_send()
+        return carry
+
+    lax.fori_loop(0, CHUNKS, collect, 0)
+    for step in range(1, n_y):
+        column_copy(step).wait_send()
+    for source in range(n_y):
+        relay_copy(source).wait_send()
+    weight_away.wait_send()
+
+
 def project_rows(row_values, w_down):
-    columns = lax.all_to_all(row_values, "img", split_axis=1, concat_axis=0, tiled=True)
-    bias_part = jnp.sum(columns.astype(jnp.float32), axis=0)
-    products = lax.psum_scatter(
-        lax.dot_general(
-            columns, w_down, (((1,), (1,)), ((), ())), preferred_element_type=jnp.float32
-        ).astype(jnp.bfloat16),
-        "img",
-        scatter_dimension=0,
-        tiled=True,
-    )
-    return products, bias_part
+    n_img = lax.axis_size("img")
+    n_y = n_img // CORES
+    hops = n_y // 2
+    rows, in_width = row_values.shape
+    out_width, block = w_down.shape
+    half = out_width // CORES
+    width = half // CHUNKS
+    chip_rows = CORES * rows
+    products, bias_sums = pl.pallas_call(
+        functools.partial(project_kernel, n_y),
+        out_shape=(
+            jax.ShapeDtypeStruct((rows, out_width), jnp.bfloat16),
+            jax.ShapeDtypeStruct((1, CORES * block), jnp.float32),
+        ),
+        in_specs=[
+            pl.BlockSpec(memory_space=pltpu.VMEM),
+            pl.BlockSpec(memory_space=pl.ANY),
+        ],
+        out_specs=(
+            pl.BlockSpec(memory_space=pltpu.VMEM),
+            pl.BlockSpec(memory_space=pltpu.VMEM),
+        ),
+        scratch_shapes=[
+            pltpu.VMEM((CORES, half, block), jnp.bfloat16),
+            pltpu.VMEM((n_img, rows, CORES * block), jnp.bfloat16),
+            pltpu.VMEM((CHUNKS, n_img * rows, width), jnp.float32),
+            pltpu.VMEM((2, CHUNKS, chip_rows, width // 2), jnp.bfloat16),
+            pltpu.VMEM((2, CHUNKS, chip_rows, width // 2), jnp.bfloat16),
+            pltpu.VMEM((2, hops - 1, CHUNKS, chip_rows, width), jnp.bfloat16),
+            pltpu.VMEM((2, hops - 1, CHUNKS, chip_rows, width), jnp.bfloat16),
+            pltpu.VMEM((CHUNKS, CORES, rows, width), jnp.bfloat16),
+            pltpu.VMEM((CHUNKS, rows, width), jnp.bfloat16),
+            pltpu.SemaphoreType.DMA((4,)),
+            pltpu.SemaphoreType.DMA((n_y,)),
+            pltpu.SemaphoreType.DMA((n_y,)),
+            pltpu.SemaphoreType.DMA((n_y,)),
+            pltpu.SemaphoreType.DMA((n_y,)),
+            pltpu.SemaphoreType.DMA((2, hops, CHUNKS)),
+            pltpu.SemaphoreType.DMA((2, hops, CHUNKS)),
+            pltpu.SemaphoreType.DMA((CHUNKS,)),
+            pltpu.SemaphoreType.DMA((CHUNKS,)),
+        ],
+        compiler_params=pltpu.CompilerParams(
+            collective_id=1, has_side_effects=True, vmem_limit_bytes=48 << 20
+        ),
+        name="project_rows",
+    )(row_values, w_down)
+    own = lax.rem(lax.axis_index("img"), CORES) * block
+    return products, lax.dynamic_slice(bias_sums[0], (own,), (block,))
 
 
 def ring_sum_kernel(

time: 201 us -> 144 us (0.72)
  waiting for transfers between devices: 79 us -> 16.2 us
  Pallas kernels: 31.7 us -> 80.9 us
  blocking collectives: 33.9 us -> 0 us
  between operations: 14.3 us -> 0.91 us
  matrix products: 13.6 us -> 4.05 us
  starting transfers between devices: 11.2 us -> 18.6 us
  local copies, waits for them, and re-layouts: 12.4 us -> 16 us
  other arithmetic: 4.19 us -> 6.71 us
    reduce_scatter x1 -> x0, waiting for transfers between devices: 66.6 us -> none  [project_rows(): lax.psum_scatter(lax.dot_general(columns, w_down, (((1,), (1,)), ((), ())...]
    pallas_call x0 -> x1, Pallas kernels: none -> 57.3 us  [project_rows(): pl.pallas_call(functools.partial(project_kernel, n_y), out_shape=(jax.Sha...]
    all_to_all x1 -> x0, blocking collectives: 33.9 us -> none  [project_rows(): lax.all_to_all(row_values, 'img', split_axis=1, concat_axis=0, tiled=True)]
    pallas_call x1, Pallas kernels: 31.7 us -> 23.6 us  [sum_terms(): pl.pallas_call(functools.partial(ring_sum_kernel, n_img, n_side, gain_row...]
    all_to_all x1, starting transfers between devices: 11.2 us -> 18.6 us  [body(): lax.all_to_all(packed, 'seq', split_axis=0, concat_axis=0, tiled=True)]
    dot_general x1 -> x0, matrix products: 7.15 us -> none  [project_rows(): lax.dot_general(columns, w_down, (((1,), (1,)), ((), ())), preferred_elem...]
    all_to_all x1, waiting for transfers between devices: 12.4 us -> 16.2 us  [body(): lax.all_to_all(packed, 'seq', split_axis=0, concat_axis=0, tiled=True)]
    unnamed x38 -> x39, local copies, waits for them, and re-layouts: 9.97 us -> 13.8 us
  transfers between devices with their start and end apart: 2 -> 1, of which waited for: 2 -> 1; matrix products, arithmetic and copies ran while one was open for 2% -> 2% of each run, Pallas kernels for 0% -> 0%
where the time goes in v2:
time: 144 us; the launch traced here: 143 us
  Pallas kernels  80.9 us (56%)
  starting transfers between devices  18.6 us (13%)
  waiting for transfers between devices  16.2 us (11%)
  local copies, waits for them, and re-layouts  16 us (11%)
  other arithmetic  6.71 us (5%)
  matrix products  4.05 us (3%)
    pallas_call x1, Pallas kernels, project_rows(): pl.pallas_call(functools.partial(project_kernel, n_y), out_shape=(jax.Sha...  57.3 us
    pallas_call x1, Pallas kernels, sum_terms(): pl.pallas_call(functools.partial(ring_sum_kernel, n_img, n_side, gain_row...  23.6 us
    all_to_all x1, starting transfers between devices, body(): lax.all_to_all(packed, 'seq', split_axis=0, concat_axis=0, tiled=True)  18.6 us
    all_to_all x1, waiting for transfers between devices, body(): lax.all_to_all(packed, 'seq', split_axis=0, concat_axis=0, tiled=True)  16.2 us
    unnamed x39, local copies, waits for them, and re-layouts  13.8 us
  transfers between devices with their start and end apart: 1, of which 1 were waited for; matrix products, arithmetic and copies ran while one was open for 2% of the time, Pallas kernels for 0%

profile of v2, /device:TPU:1, one launch (start us, length us, event | category | flops | bytes accessed | tf_op | source)
XLA Modules:
  0.0 143.4 jit_solution(10749799881805632362)
XLA Ops:
  0.6 0.7 fusion.25
  1.3 0.7 and_select_fusion.1
  2.0 0.7 fusion.44
  2.6 0.2 convert_reduce_fusion
  2.8 0.7 fusion.26
  3.5 2.5 %copy-done = bf16[5120,512]{1,0:T(8,128)(2,1)S(1)} copy-done((bf16[5120,512]{1,0:T(8,128)(2,1)S(1)}, bf16[5120,512]{1,0:T(8,128)(2,1)}, u32[]{:S(2)}) %copy-start) | copy-done | bytes 5242904
  6.0 1.0 copy-done.1
  7.0 57.3 %project_rows.1 = (bf16[32,5120]{1,0:T(8,128)(2,1)S(1)}, f32[1,1024]{1,0:T(1,128)S(1)}) custom-call(bf16[32,8192]{1,0:T(8,128)(2,1)S(1)} %bitcast.81, bf16[5120,512]{1,0:T(8,128)(2,1)S(1)} %copy-done), custom_call_target="tpu_custom_call" | custom-call | tf_op jit(solution)/shard_map/project_rows/pallas_call | solution.py:324
  64.3 0.1 broadcast_in_dim.15
  64.4 0.3 fusion.1
  64.7 0.5 broadcast.202
  65.2 1.1 reduce.2
  66.3 0.0 copy-start.2
  66.3 1.6 %reshape.215 = bf16[64,2,2624]{2,1,0:T(2,128)(2,1)} reshape(bf16[64,5248]{1,0:T(8,128)(2,1)S(1)} %reduce.2) | data formatting | bytes 1343488
  67.9 18.6 %all-to-all-start = ((bf16[64,2,2624]{2,1,0:T(2,128)(2,1)}), bf16[64,2,2624]{2,1,0:T(2,128)(2,1)S(1)}, u32[]{:S(2)}, u32[]{:S(2)}) async-start(bf16[64,2,2624]{2,1,0:T(2,128)(2,1)} %reshape.215), calls=%async_computation | async-start | bytes 1376256 | tf_op jit(solution)/shard_map/all_to_all | solution.py:530
  86.5 0.0 copy-start.12
  86.5 0.0 copy-start.9
  86.6 0.0 copy-done.2
  86.6 0.2 copy.75
  86.7 0.0 copy-done.11
  86.7 0.1 mul.80
  86.8 0.0 copy-done.7
  86.8 0.2 copy.71
  87.1 0.0 copy-done.8
  87.1 0.0 copy-start.5
  87.1 0.2 copy.72
  87.3 0.0 copy-start.3
  87.3 0.0 copy-done.12
  87.3 0.1 broadcast_in_dim.12
  87.4 0.1 eq.64
  87.5 0.9 copy.76
  88.4 0.1 fusion.13
  88.6 0.1 broadcast_compare_fusion
  88.7 1.5 %fusion.33 = (f32[16,128]{1,0:T(8,128)S(1)}, f32[16,128,128]{1,2,0:T(8,128)}) fusion(bf16[128,16,80]{0,2,1:T(8,128)(2,1)S(1)} %bitcast.87, bf16[128,16,80]{0,2,1:T(8,128)(2,1)S(1)} %bitcast.85, pred[128,128]{0,1:T(8,128)(4,1)S(1)} %broadcast_compare_fusion), kind=kOutput, calls=%fused_computation.72 | convolution fusion | flops 42991744 | bytes 1728512 | tf_op jit(solution)/shard_map/sub | solution.py:495
  90.2 0.0 copy-done.5
  90.2 16.2 %all-to-all-done = bf16[64,2,2624]{2,1,0:T(2,128)(2,1)S(1)} async-done(((bf16[64,2,2624]{2,1,0:T(2,128)(2,1)}), bf16[64,2,2624]{2,1,0:T(2,128)(2,1)S(1)}, u32[]{:S(2)}, u32[]{:S(2)}) %all-to-all-start) | async-done | bytes 671776 | tf_op jit(solution)/shard_map/all_to_all | solution.py:530
  106.4 1.0 reshape.216
  107.4 0.1 copy.95
  107.5 0.1 add_reduce_fusion
  107.6 0.2 fusion.2
  107.8 0.2 reshape.213
  108.0 0.5 reshape.211
  108.6 0.3 multiply_reduce_fusion
  108.9 0.0 copy-start.10
  108.9 0.4 copy.74
  109.3 0.2 multiply_convert_fusion
  109.6 0.3 copy-done.10
  109.9 0.7 copy-done.13
  110.6 0.3 fusion.11
  110.9 0.0 copy-start.6
  110.9 0.4 fusion.7
  111.3 0.6 copy-done.6
  111.9 0.5 fusion.9
  112.4 0.5 copy-done.4
  112.9 0.3 fusion.10
  113.2 0.5 convolution_convert_fusion.2
  113.7 0.6 fusion.21.terms
  114.3 23.6 %sum_terms.1 = (f32[16,128]{1,0:T(8,128)}, f32[16,8,128]{2,1,0:T(8,128)}) custom-call(f32[24,128]{1,0:T(8,128)} %fusion.21.terms), custom_call_target="tpu_custom_call" | custom-call | tf_op jit(solution)/shard_map/sum_terms/pallas_call | solution.py:453
  137.9 0.9 copy.96
  138.8 0.6 copy.92
  139.4 1.3 multiply_bitcast_fusion
  140.7 0.9 copy.83
  141.6 0.9 copy.82
  142.5 0.9 copy.84
  (13 shorter events, 0.0 us)
Async XLA Ops:
  3.5 2.5 %copy-start = (bf16[5120,512]{1,0:T(8,128)(2,1)S(1)}, bf16[5120,512]{1,0:T(8,128)(2,1)}, u32[]{:S(2)}) copy-start(bf16[5120,512]{1,0:T(8,128)(2,1)} %w_down.1) | copy-start | bytes 15728644
  6.0 1.0 copy-start.1
  66.3 20.3 %copy-start.2 = (bf16[1,128,1280]{2,1,0:T(8,128)(2,1)S(1)}, bf16[1,128,1280]{2,1,0:T(8,128)(2,1)}, u32[]{:S(2)}) copy-start(bf16[1,128,1280]{2,1,0:T(8,128)(2,1)} %param.11) | copy-start | bytes 983044
  67.9 18.9 %copy-start.11 = (f32[1280]{0:T(1024)S(1)}, f32[1280]{0:T(1024)}, u32[]{:S(2)}) copy-start(f32[1280]{0:T(1024)} %param.12) | copy-start | bytes 15364
  67.9 18.9 %copy-start.7 = (bf16[1,128,1280]{2,1,0:T(8,128)(2,1)S(1)}, bf16[1,128,1280]{2,1,0:T(8,128)(2,1)}, u32[]{:S(2)}) copy-start(bf16[1,128,1280]{2,1,0:T(8,128)(2,1)} %param.14) | copy-start | bytes 983044
  67.9 19.2 %copy-start.8 = (bf16[1,128,1280]{2,1,0:T(8,128)(2,1)S(1)}, bf16[1,128,1280]{2,1,0:T(8,128)(2,1)}, u32[]{:S(2)}) copy-start(bf16[1,128,1280]{2,1,0:T(8,128)(2,1)} %param.15) | copy-start | bytes 983044
  67.9 38.5 %all-to-all-start = ((bf16[64,2,2624]{2,1,0:T(2,128)(2,1)}), bf16[64,2,2624]{2,1,0:T(2,128)(2,1)S(1)}, u32[]{:S(2)}, u32[]{:S(2)}) async-start(bf16[64,2,2624]{2,1,0:T(2,128)(2,1)} %reshape.215), calls=%async_computation | async-start | bytes 1376256 | tf_op jit(solution)/shard_map/all_to_all | solution.py:530
  86.5 0.8 copy-start.12
  86.5 1.0 copy-start.9
  87.1 3.1 %copy-start.5 = (bf16[1,128,1280]{1,2,0:T(8,128)(2,1)}, bf16[1,128,1280]{1,2,0:T(8,128)(2,1)S(1)}, u32[]{:S(2)}) copy-start(bf16[1,128,1280]{1,2,0:T(8,128)(2,1)S(1)} %copy.71) | copy-start | bytes 983044
  87.3 2.9 %copy-start.3 = (bf16[1,128,1280]{1,2,0:T(8,128)(2,1)}, bf16[1,128,1280]{1,2,0:T(8,128)(2,1)S(1)}, u32[]{:S(2)}) copy-start(bf16[1,128,1280]{1,2,0:T(8,128)(2,1)S(1)} %copy.72) | copy-start | bytes 983044
  108.9 1.0 copy-start.10
  109.3 1.2 copy-start.13
  110.9 1.0 copy-start.6
  111.9 1.0 copy-start.4

commit v3 on v2

--- a/solution.py
+++ b/solution.py
@@ -12,36 +12,37 @@
 HEAD_DIM = 80
 
 
-def earlier_equal(labels, order_key):
-    same_label = labels[:, None] == labels[None, :]
-    earlier = order_key[None, :] < order_key[:, None]
-    return jnp.sum(jnp.logical_and(same_label, earlier), axis=1)
-
-
-def pack_rows(row_values, targets, peer_count, capacity):
-    row_count = row_values.shape[0]
+FOLD = 8
+
+
+def route_tables(targets, peer_count):
+    row_count = targets.shape[0]
     destination = targets // row_count
-    local_row = (targets % row_count).astype(jnp.float32).astype(row_values.dtype)
-    slot_index = destination * capacity + earlier_equal(
-        destination, jnp.arange(row_count, dtype=jnp.int32)
-    )
-    matches = slot_index[None, :] == jnp.arange(peer_count * capacity, dtype=jnp.int32)[:, None]
-    selector = matches.astype(row_values.dtype)
-    labelled = jnp.concatenate(
-        [row_values, jnp.broadcast_to(local_row[:, None] + 1, (row_count, 128))], axis=1
-    )
-    return jnp.dot(selector, labelled, preferred_element_type=jnp.float32).astype(row_values.dtype)
-
-
-def unpack_rows(received, row_count):
-    width = received.shape[1] - 128
-    labels = received[:, width].astype(jnp.float32).astype(jnp.int32) - 1
-    selector = (labels[None, :] == jnp.arange(row_count, dtype=jnp.int32)[:, None]).astype(
-        received.dtype
-    )
-    return jnp.dot(
-        selector, received[:, :width], preferred_element_type=jnp.float32
-    ).astype(received.dtype)
+    local_row = targets % row_count
+    matches = destination[None, :] == jnp.arange(peer_count, dtype=jnp.int32)[:, None]
+    labels = jnp.sum(jnp.where(matches, local_row[None, :] + 1, 0), axis=1)
+    slot_of = lax.broadcasted_iota(jnp.int32, (peer_count * FOLD, FOLD * row_count), 0)
+    fold_of = lax.broadcasted_iota(jnp.int32, (peer_count * FOLD, FOLD * row_count), 1)
+    selector = jnp.logical_and(
+        slot_of // FOLD == jnp.tile(destination, FOLD)[None, :],
+        slot_of % FOLD == fold_of // row_count,
+    ).astype(jnp.bfloat16)
+    labels = jnp.broadcast_to(labels.astype(jnp.int32)[:, None, None], (peer_count, 1, 128))
+    return selector, labels
+
+
+def place_patches(arrived, labels, row_count, patches_per_row):
+    peer_count, _, piece = arrived.shape
+    pieces = FOLD // patches_per_row
+    flat = arrived.reshape(peer_count * FOLD, piece)
+    wanted = (labels[:, None] - 1) * FOLD + jnp.arange(FOLD, dtype=jnp.int32)[None, :]
+    wanted = wanted.reshape(-1)
+    patch = jnp.arange(row_count * patches_per_row, dtype=jnp.int32)
+    columns = []
+    for at in range(pieces):
+        selector = (wanted[None, :] == (patch * pieces + at)[:, None]).astype(flat.dtype)
+        columns.append(jnp.dot(selector, flat, preferred_element_type=jnp.float32))
+    return jnp.concatenate(columns, axis=1)
 
 
 CORES = 2
@@ -51,10 +52,18 @@
 
 def project_kernel(
     n_y,
+    n_side,
     grads,
     w_down,
+    selector,
+    labels,
+    arrived_out,
+    labels_out,
+    bias_part,
     products,
-    bias_part,
+    packed,
+    arrived,
+    label_slots,
     weights,
     columns,
     parts,
@@ -73,6 +82,10 @@
     ring_recv,
     swap_send,
     swap_recv,
+    label_send,
+    label_recv,
+    route_send,
+    route_recv,
 ):
     img = lax.axis_index("img")
     seq = lax.axis_index("seq")
@@ -91,6 +104,65 @@
         return (there * CORES + which, seq)
 
     twin = at_chip(y, other)
+    n_seq = n_side * n_side
+    high = seq // n_side
+    low = lax.rem(seq, n_side)
+
+    def ahead(step):
+        return (
+            lax.rem(high + step // n_side, n_side) * n_side
+            + lax.rem(low + lax.rem(step, n_side), n_side)
+        )
+
+    def behind(step):
+        return (
+            lax.rem(high + n_side - step // n_side, n_side) * n_side
+            + lax.rem(low + n_side - lax.rem(step, n_side), n_side)
+        )
+
+    def label_copy(step):
+        target = ahead(step)
+        return pltpu.make_async_remote_copy(
+            src_ref=labels.at[target],
+            dst_ref=label_slots.at[seq],
+            send_sem=label_send.at[step],
+            recv_sem=label_recv.at[step],
+            device_id=(img, target),
+            device_id_type=MESH,
+        )
+
+    def route_copy(step):
+        target = ahead(step)
+        return pltpu.make_async_remote_copy(
+            src_ref=packed.at[target],
+            dst_ref=arrived.at[seq],
+            send_sem=route_send.at[step],
+            recv_sem=route_recv.at[step],
+            device_id=(img, target),
+            device_id_type=MESH,
+        )
+
+    def label_arrival(step):
+        source = behind(step)
+        return pltpu.make_async_remote_copy(
+            src_ref=labels.at[source],
+            dst_ref=label_slots.at[source],
+            send_sem=label_send.at[step],
+            recv_sem=label_recv.at[step],
+            device_id=(img, source),
+            device_id_type=MESH,
+        )
+
+    def route_arrival(step):
+        source = behind(step)
+        return pltpu.make_async_remote_copy(
+            src_ref=packed.at[source],
+            dst_ref=arrived.at[source],
+            send_sem=route_send.at[step],
+            recv_sem=route_recv.at[step],
+            device_id=(img, source),
+            device_id_type=MESH,
+        )
 
     barrier = pltpu.get_barrier_semaphore()
     pl.semaphore_signal(barrier, inc=1, device_id=twin, device_id_type=MESH)
@@ -101,7 +173,13 @@
             device_id=at_chip(lax.rem(y + step, n_y), core),
             device_id_type=MESH,
         )
-    pl.semaphore_wait(barrier, n_y)
+
+    def greet(step, carry):
+        pl.semaphore_signal(barrier, inc=1, device_id=(img, ahead(step)), device_id_type=MESH)
+        return carry
+
+    lax.fori_loop(1, n_seq, greet, 0)
+    pl.semaphore_wait(barrier, n_y + n_seq - 1)
 
     def column_copy(step):
         target = lax.rem(y + step, n_y)
@@ -174,6 +252,13 @@
         weight_sem.at[3],
     )
     own_columns.start()
+
+    def send_label(step, carry):
+        label_copy(step).start()
+        return carry
+
+    lax.fori_loop(1, n_seq, send_label, 0)
+    label_slots[seq] = labels[seq]
     own_columns.wait()
     relay_copy(y).start()
     for step in reversed(outward):
@@ -305,15 +390,45 @@
         return carry
 
     lax.fori_loop(0, CHUNKS, collect, 0)
+
+    piece = packed.shape[2]
+    folded = jnp.concatenate(
+        [products[:, at * piece : (at + 1) * piece] for at in range(FOLD)], axis=0
+    )
+    packed[...] = (
+        jnp.dot(selector[...], folded, preferred_element_type=jnp.float32)
+        .reshape(n_seq, FOLD, piece)
+        .astype(jnp.bfloat16)
+    )
+
+    def send_row(step, carry):
+        route_copy(step).start()
+        return carry
+
+    lax.fori_loop(1, n_seq, send_row, 0)
+    arrived[seq] = packed[seq]
     for step in range(1, n_y):
         column_copy(step).wait_send()
     for source in range(n_y):
         relay_copy(source).wait_send()
     weight_away.wait_send()
 
-
-def project_rows(row_values, w_down):
+    def settle(step, carry):
+        label_arrival(step).wait_recv()
+        label_copy(step).wait_send()
+        route_arrival(step).wait_recv()
+        route_copy(step).wait_send()
+        return carry
+
+    lax.fori_loop(1, n_seq, settle, 0)
+    arrived_out[...] = arrived[...]
+    labels_out[...] = label_slots[...]
+
+
+def project_rows(row_values, w_down, selector, labels):
     n_img = lax.axis_size("img")
+    n_seq = lax.axis_size("seq")
+    n_side = math.isqrt(n_seq)
     n_y = n_img // CORES
     hops = n_y // 2
     rows, in_width = row_values.shape
@@ -321,21 +436,29 @@
     half = out_width // CORES
     width = half // CHUNKS
     chip_rows = CORES * rows
-    products, bias_sums = pl.pallas_call(
-        functools.partial(project_kernel, n_y),
+    arrived, arrived_labels, bias_sums = pl.pallas_call(
+        functools.partial(project_kernel, n_y, n_side),
         out_shape=(
-            jax.ShapeDtypeStruct((rows, out_width), jnp.bfloat16),
+            jax.ShapeDtypeStruct((n_seq, FOLD, out_width // FOLD), jnp.bfloat16),
+            jax.ShapeDtypeStruct((n_seq, 1, 128), jnp.int32),
             jax.ShapeDtypeStruct((1, CORES * block), jnp.float32),
         ),
         in_specs=[
             pl.BlockSpec(memory_space=pltpu.VMEM),
-            pl.BlockSpec(memory_space=pl.ANY),
+            pl.BlockSpec(memory_space=pltpu.HBM),
+            pl.BlockSpec(memory_space=pltpu.VMEM),
+            pl.BlockSpec(memory_space=pltpu.VMEM),
         ],
         out_specs=(
             pl.BlockSpec(memory_space=pltpu.VMEM),
             pl.BlockSpec(memory_space=pltpu.VMEM),
+            pl.BlockSpec(memory_space=pltpu.VMEM),
         ),
         scratch_shapes=[
+            pltpu.VMEM((rows, out_width), jnp.bfloat16),
+            pltpu.VMEM((n_seq, FOLD, out_width // FOLD), jnp.bfloat16),
+            pltpu.VMEM((n_seq, FOLD, out_width // FOLD), jnp.bfloat16),
+            pltpu.VMEM((n_seq, 1, 128), jnp.int32),
             pltpu.VMEM((CORES, half, block), jnp.bfloat16),
             pltpu.VMEM((n_img, rows, CORES * block), jnp.bfloat16),
             pltpu.VMEM((CHUNKS, n_img * rows, width), jnp.float32),
@@ -354,14 +477,19 @@
             pltpu.SemaphoreType.DMA((2, hops, CHUNKS)),
             pltpu.SemaphoreType.DMA((CHUNKS,)),
             pltpu.SemaphoreType.DMA((CHUNKS,)),
+            pltpu.SemaphoreType.DMA((n_seq,)),
+            pltpu.SemaphoreType.DMA((n_seq,)),
+            pltpu.SemaphoreType.DMA((n_seq,)),
+            pltpu.SemaphoreType.DMA((n_seq,)),
         ],
         compiler_params=pltpu.CompilerParams(
             collective_id=1, has_side_effects=True, vmem_limit_bytes=48 << 20
         ),
         name="project_rows",
-    )(row_values, w_down)
+    )(row_values, w_down, selector, labels)
     own = lax.rem(lax.axis_index("img"), CORES) * block
-    return products, lax.dynamic_slice(bias_sums[0], (own,), (block,))
+    bias_part = lax.dynamic_slice(bias_sums[0], (own,), (block,))
+    return arrived, arrived_labels[:, 0, 0], bias_part
 
 
 def ring_sum_kernel(
@@ -524,13 +652,12 @@
     targets = token_target[0]
     row_count = grad_rows.shape[0]
     peer_count = lax.axis_size("seq")
-    capacity = max(1, 2 * row_count // peer_count)
-    products, bias_part = project_rows(grad_rows, w_down)
-    packed = pack_rows(products, targets, peer_count, capacity)
-    arrived = lax.all_to_all(packed, "seq", split_axis=0, concat_axis=0, tiled=True)
-    merged = unpack_rows(arrived, row_count)
     patch_width = patches.shape[2]
-    patch_grads = merged.reshape(-1, patch_width).astype(jnp.float32)
+    selector, labels = route_tables(targets, peer_count)
+    arrived, arrived_labels, bias_part = project_rows(grad_rows, w_down, selector, labels)
+    patch_grads = place_patches(
+        arrived, arrived_labels, row_count, w_down.shape[0] // patch_width
+    )
     inputs = patches[0].astype(jnp.float32)
     inverse_rms = lax.rsqrt(jnp.mean(inputs * inputs, axis=1, keepdims=True) + 1e-06)
     normed = inputs * inverse_rms

time: 144 us -> 135 us (0.938)
  Pallas kernels: 80.9 us -> 117 us
  starting transfers between devices: 18.6 us -> 0 us
  waiting for transfers between devices: 16.2 us -> 0 us
  local copies, waits for them, and re-layouts: 16 us -> 8.02 us
    pallas_call x1, Pallas kernels: 57.3 us -> 92.2 us  [project_rows(): pl.pallas_call(functools.partial(project_kernel, n_y, n_side), out_shape=...]
    all_to_all x1 -> x0, starting transfers between devices: 18.6 us -> none  [body(): lax.all_to_all(packed, 'seq', split_axis=0, concat_axis=0, tiled=True)]
    all_to_all x1 -> x0, waiting for transfers between devices: 16.2 us -> none  [body(): lax.all_to_all(packed, 'seq', split_axis=0, concat_axis=0, tiled=True)]
    unnamed x39 -> x20, local copies, waits for them, and re-layouts: 13.8 us -> 6.97 us
    pallas_call x1, Pallas kernels: 23.6 us -> 25.1 us  [sum_terms(): pl.pallas_call(functools.partial(ring_sum_kernel, n_img, n_side, gain_row...]
  transfers between devices with their start and end apart: 1 -> 0, of which waited for: 1 -> 0; matrix products, arithmetic and copies ran while one was open for 2% -> 0% of each run, Pallas kernels for 0% -> 0%
where the time goes in v3:
time: 135 us
  Pallas kernels  117 us (87%)
  local copies, waits for them, and re-layouts  8.02 us (6%)
  other arithmetic  5.44 us (4%)
  matrix products  3.17 us (2%)
    pallas_call x1, Pallas kernels, project_rows(): pl.pallas_call(functools.partial(project_kernel, n_y, n_side), out_shape=...  92.2 us
    pallas_call x1, Pallas kernels, sum_terms(): pl.pallas_call(functools.partial(ring_sum_kernel, n_img, n_side, gain_row...  25.1 us
    unnamed x20, local copies, waits for them, and re-layouts  6.97 us

profile of v3, /device:TPU:1, one launch (start us, length us, event | category | flops | bytes accessed | tf_op | source)
XLA Modules:
  0.0 134.7 jit_solution(10214729276838441851)
XLA Ops:
  0.6 0.0 copy-start.1
  0.6 1.2 copy.46
  1.9 0.7 fusion.36
  2.6 0.1 eq.77
  2.7 0.6 fusion.19.selector
  3.3 0.1 select_reduce_fusion
  3.4 0.1 broadcast_in_dim.36.labels
  3.6 0.0 copy-start
  3.6 1.0 copy-done
  4.6 0.0 copy-start.4
  4.6 0.0 copy-start.2
  4.6 92.2 %project_rows.1 = (bf16[64,8,640]{2,1,0:T(8,128)(2,1)S(1)}, s32[64,1,128]{2,1,0:T(1,128)S(1)}, f32[1,1024]{1,0:T(1,128)S(1)}) custom-call(bf16[32,8192]{1,0:T(8,128)(2,1)S(1)} %bitcast.64, bf16[5120,512]{1,0:T(8,128)(2,1)} %w_down.1, bf16[512,256]{1,0:T(8,128)(2,1)S(1)} %fusion.19.selector, s32[64,1,128]{2,1,0:T(1,128)S(1)} %broadcast_in_dim.36.labels), custom_call_target="tpu_custom_call" | custom-call | tf_op jit(solution)/shard_map/project_rows/pallas_call | solution.py:439
  96.8 0.0 copy-start.3
  96.8 0.0 copy-start.5
  96.8 1.2 multiply_reduce_fusion.2
  98.0 0.1 iota_add_fusion
  98.1 0.1 add.89
  98.2 0.3 fusion.13
  98.6 0.2 copy.48
  98.7 0.3 fusion.15
  99.1 0.2 copy.47
  99.2 0.0 copy-done.1
  99.2 0.2 copy.49
  99.4 0.1 fusion.17
  99.6 0.0 copy-done.4
  99.6 0.3 multiply_reduce_fusion
  99.9 0.1 mul.107
  99.9 0.3 fusion.12
  100.2 0.0 copy-done.2
  100.2 0.2 copy.50
  100.4 0.0 copy-done.3
  100.4 0.2 copy.45
  100.7 0.0 copy-done.5
  100.7 0.1 broadcast_in_dim.26
  100.8 0.1 eq.73
  100.9 0.1 broadcast_compare_fusion
  101.0 0.5 fusion.43
  101.5 0.3 fusion.9
  101.8 0.4 fusion.5
  102.2 0.3 fusion.8
  102.6 0.9 copy.56
  103.5 0.5 fusion.7
  104.0 0.9 copy.57
  104.9 0.5 convolution_convert_fusion
  105.4 0.9 copy.58
  106.3 0.6 fusion.28.terms
  106.9 25.1 %sum_terms.1 = (f32[16,128]{1,0:T(8,128)}, f32[16,8,128]{2,1,0:T(8,128)}) custom-call(f32[24,128]{1,0:T(8,128)} %fusion.28.terms), custom_call_target="tpu_custom_call" | custom-call | tf_op jit(solution)/shard_map/sum_terms/pallas_call | solution.py:581
  132.0 1.3 multiply_bitcast_fusion
  133.3 0.9 copy.67
  134.1 0.6 copy.65
  (12 shorter events, 0.1 us)
Async XLA Ops:
  0.6 98.6 %copy-start.1 = (bf16[1,128,1280]{2,1,0:T(8,128)(2,1)S(1)}, bf16[1,128,1280]{2,1,0:T(8,128)(2,1)}, u32[]{:S(2)}) copy-start(bf16[1,128,1280]{2,1,0:T(8,128)(2,1)} %param.11) | copy-start | bytes 983044
  3.6 1.0 copy-start
  4.6 94.9 %copy-start.4 = (f32[1280]{0:T(1024)S(1)}, f32[1280]{0:T(1024)}, u32[]{:S(2)}) copy-start(f32[1280]{0:T(1024)} %param.12) | copy-start | bytes 15364
  4.6 95.6 %copy-start.2 = (bf16[1,128,1280]{2,1,0:T(8,128)(2,1)S(1)}, bf16[1,128,1280]{2,1,0:T(8,128)(2,1)}, u32[]{:S(2)}) copy-start(bf16[1,128,1280]{2,1,0:T(8,128)(2,1)} %param.16) | copy-start | bytes 983044
  96.8 3.6 %copy-start.3 = (bf16[1,128,1280]{2,1,0:T(8,128)(2,1)S(1)}, bf16[1,128,1280]{2,1,0:T(8,128)(2,1)}, u32[]{:S(2)}) copy-start(bf16[1,128,1280]{2,1,0:T(8,128)(2,1)} %param.14) | copy-start | bytes 983044
  96.8 3.9 %copy-start.5 = (s32[1,1,32]{2,1,0:T(1,128)S(1)}, s32[1,1,32]{2,1,0:T(1,128)}, u32[]{:S(2)}) copy-start(s32[1,1,32]{2,1,0:T(1,128)} %param.17) | copy-start | bytes 388
